TPU v7x, 32 devices: a whole 2x2x4 slice. The times are simulated.
32 devices in a mesh: dom: 16 (over z, x, core), col: 2 (over y).
Axes of the slice: x: 2, y: 2, z: 4, core: 2. Of those that a mesh axis runs over, the one named last changes fastest.
Arguments:
- feats: bfloat16 [8192, 256], P('dom', 'col'), may hold values from -6 to 6
- w_first: bfloat16 [256, 256], replicated, may hold values from -0.375 to 0.375
- w_second: bfloat16 [256, 256], replicated, may hold values from -0.375 to 0.375
- block_cols: int32 [64, 32], P('dom'), may hold values from 0 to 63, as said below
- block_count: int32 [64], P('dom'), may hold values from 1 to 32
- block_vals: bfloat16 [64, 32, 128, 128], P('dom', 'col'), may hold values from -0.125 to 0.125
- cotangent: bfloat16 [8192, 256], P('dom', 'col'), may hold values from -6 to 6
Outputs:
- output: float32 [8192, 256], P('dom', 'col')
- grad_first: float32 [256, 256], P(None, 'col')
- grad_second: float32 [256, 256], P(None, 'col')
Inputs may be any that keep to these rules, and one draw needn't show every extreme that they name: Each row of block_cols names 32 different column blocks.
All inputs are finite; a program needn't handle non-finite values.
Results may differ from a plain program's by a relative error of at most 0.019.
Values may be sent and summed in bfloat16 or wider, within the bound.
No kernel may reach another device: no remote copies, remote signals or barrier semaphores. Data moves between devices by JAX's collectives and lax.ppermute only.
A program may use at most 64 MiB of HBM per device.

v0:
```python
import jax
import jax.numpy as jnp
from jax import lax
from jax.sharding import PartitionSpec as P

BLK = 128


def silu_slope(value):
    sig = jax.nn.sigmoid(value)
    return sig + value * sig * (1.0 - sig)


def forward_fold(prod, cols, vals):
    rows, width = prod.shape
    piece = lax.all_gather(prod, "dom", axis=0, tiled=True)
    count_blocks = piece.shape[0] // BLK
    hit = (cols >= 0) & (cols < count_blocks)
    picked = piece.reshape(count_blocks, BLK, width)[jnp.clip(cols, 0, count_blocks - 1)]
    picked = jnp.where(hit[:, :, None, None], picked, jnp.zeros((), picked.dtype))
    contrib = jnp.einsum("rkij,rkjf->rif", vals, picked, preferred_element_type=jnp.float32)
    return contrib.reshape(rows, width)


def backward_scatter(grad, cols, vals):
    rows, width = grad.shape
    nblocks = rows // BLK
    products = jnp.einsum(
        "rkij,rif->rkjf",
        vals,
        grad.reshape(nblocks, BLK, width),
        preferred_element_type=jnp.float32,
    )
    count = rows * lax.axis_size("dom")
    count_blocks = count // BLK
    onehot = (cols[:, :, None] == jnp.arange(count_blocks)[None, None, :]).astype(jnp.float32)
    summed = jnp.einsum("rkp,rkjf->pjf", onehot, products, precision=lax.Precision.HIGHEST)
    return lax.psum_scatter(summed.reshape(count, width), "dom", scatter_dimension=0, tiled=True)


def body(feats, w_first, w_second, block_cols, block_count, block_vals, cotangent):
    col_index = lax.axis_index("col")
    rows, narrow = feats.shape

    def widen(value):
        return lax.all_gather(value, "col", axis=1, tiled=True)

    def weight_grad(full, back):
        return lax.psum(
            jnp.dot(full.T, back, preferred_element_type=jnp.float32).astype(jnp.bfloat16), "dom"
        ).astype(jnp.float32)

    all_vals = lax.all_gather(block_vals, "col", axis=1, tiled=True)
    slot_ids = jnp.arange(all_vals.shape[1])
    usable = slot_ids[None, :] < block_count[:, None]
    vals = jnp.where(usable[:, :, None, None], all_vals, jnp.zeros((), all_vals.dtype))

    def project(full, weight):
        weight_cols = lax.dynamic_slice_in_dim(weight, col_index * narrow, narrow, 1)
        return jnp.dot(full, weight_cols, preferred_element_type=jnp.float32).astype(jnp.bfloat16)

    def aggregate(prod):
        return forward_fold(prod, block_cols, vals)

    def transpose(grad):
        return backward_scatter(grad, block_cols, vals)

    full_input = widen(feats)
    first = aggregate(project(full_input, w_first))
    hidden = (first * jax.nn.sigmoid(first)).astype(jnp.bfloat16)
    full_hidden = widen(hidden)
    output = aggregate(project(full_hidden, w_second))
    back_second = transpose(cotangent).astype(jnp.bfloat16)
    grad_second = weight_grad(full_hidden, back_second)
    second_cols = lax.dynamic_slice_in_dim(w_second, col_index * narrow, narrow, 1)
    partial_hidden = jnp.dot(back_second, second_cols.T, preferred_element_type=jnp.float32)
    hidden_grad = lax.psum_scatter(partial_hidden, "col", scatter_dimension=1, tiled=True)
    act_grad = (hidden_grad * silu_slope(first)).astype(jnp.bfloat16)
    back_first = transpose(act_grad).astype(jnp.bfloat16)
    grad_first = weight_grad(full_input, back_first)
    return (output, grad_first, grad_second)


def solution(mesh):
    in_specs = (
        P("dom", "col"),
        P(),
        P(),
        P("dom", None),
        P("dom"),
        P("dom", "col", None, None),
        P("dom", "col"),
    )
    out_specs = (P("dom", "col"), P(None, "col"), P(None, "col"))
    return jax.shard_map(body, mesh=mesh, in_specs=in_specs, out_specs=out_specs, check_vma=False)
```

profile of v0, /device:TPU:8, one launch (start us, length us, event | category | flops | bytes accessed | tf_op | source)
XLA Modules:
  0.0 452.0 jit_solution(4109258928189561779)
XLA Ops:
  8.7 58.8 %all-gather.4.cloned.1.call-done = bf16[4,32,128,128]{3,2,1,0:T(8,128)(2,1)} async-done(((bf16[4,16,128,128]{3,2,1,0:T(8,128)(2,1)}), bf16[4,32,128,128]{3,2,1,0:T(8,128)(2,1)}) %all-gather.4.cloned.1.call-update) | async-done | bytes 4194320 | tf_op jit(solution)/shard_map/all_gather | solution.py:53
  67.4 4.5 broadcast_select_fusion
  71.9 7.9 %copy.18 = bf16[4,32,128,128]{2,1,0,3:T(8,128)(2,1)} copy(bf16[4,32,128,128]{3,2,1,0:T(8,128)(2,1)} %broadcast_select_fusion) | data formatting | bytes 8388608 | tf_op jit(solution)/shard_map/jit(_where)/select_n | solution.py:56
  79.9 3.4 fusion.31
  83.3 3.9 convolution_bitcast_fusion.1
  87.3 4.4 copy.13
  92.6 5.8 %all_gather.16 = bf16[512,256]{1,0:T(8,128)(2,1)S(1)} all-gather(bf16[512,128]{1,0:T(8,128)(2,1)S(1)} %copy-done.2), channel_id=1, replica_groups=mesh['dom'=16,'col'=2] {'col'}, dimensions={1}, use_global_device_ids=true | all-gather | bytes 393216 | tf_op jit(solution)/shard_map/all_gather | solution.py:46
  99.3 64.6 %reduce-scatter.4.cloned.1.call-done = f32[512,128]{1,0:T(8,128)} async-done(((f32[8192,128]{1,0:T(8,128)}), f32[512,128]{1,0:T(8,128)}) %reduce-scatter.4.cloned.1.call-update) | async-done | bytes 262160 | tf_op jit(solution)/shard_map/reduce_scatter | solution.py:38
  163.9 2.0 fusion.16
  166.1 40.7 %all-gather.6.cloned.1.call-done = bf16[8192,128]{0,1:T(8,128)(2,1)} async-done(((bf16[512,128]{0,1:T(8,128)(2,1)}), bf16[8192,128]{0,1:T(8,128)(2,1)}) %all-gather.6.cloned.1.call-update) | async-done | bytes 2097168 | tf_op jit(solution)/shard_map/all_gather | solution.py:16
  206.8 3.2 copy.21
  210.0 3.0 gather_fusion
  213.0 5.0 %fusion.2 = f32[4,128,128,1]{2,1,3,0:T(8,128)S(1)} fusion(bf16[4,32,128,128]{3,2,1,0:T(8,128)(2,1)} %broadcast_select_fusion, bf16[4,32,128,128]{3,2,1,0:T(8,128)(2,1)} %bitcast.68, pred[4,32]{1,0:T(4,128)(4,1)S(1)} %compare_and_fusion), kind=kOutput, calls=%fused_computation.4 | convolution fusion | flops 538968064 | bytes 8650880 | tf_op jit(solution)/shard_map/rkij,rkjf->rif/dot_general | solution.py:21
  218.0 5.3 %reduce-scatter.6.cloned.1.call-done = f32[512,128]{1,0:T(8,128)} async-done(((f32[512,256]{1,0:T(8,128)}), f32[512,128]{1,0:T(8,128)}) %reduce-scatter.6.cloned.1.call-update) | async-done | bytes 262160 | tf_op jit(solution)/shard_map/reduce_scatter | solution.py:77
  224.4 5.8 %all_gather.18 = bf16[512,256]{1,0:T(8,128)(2,1)S(1)} all-gather(bf16[512,128]{1,0:T(8,128)(2,1)S(1)} %get-tuple-element.12), channel_id=1, replica_groups=mesh['dom'=16,'col'=2] {'col'}, dimensions={1}, use_global_device_ids=true | all-gather | bytes 393216 | tf_op jit(solution)/shard_map/all_gather | solution.py:46
  231.3 3.4 fusion.32
  234.8 3.9 convolution_bitcast_fusion
  238.7 4.4 copy.14
  245.0 26.6 %all-gather.8.cloned.1.call-done = bf16[8192,128]{1,0:T(8,128)(2,1)} async-done(((bf16[512,128]{1,0:T(8,128)(2,1)}), bf16[8192,128]{1,0:T(8,128)(2,1)}) %all-gather.8.cloned.1.call-update) | async-done | bytes 2097168 | tf_op jit(solution)/shard_map/all_gather | solution.py:16
  271.6 4.7 %gather_fusion.1 = bf16[128,128,128]{2,1,0:T(8,128)(2,1)} fusion(bf16[64,128,128]{2,1,0:T(8,128)(2,1)} %bitcast.66, s32[1024]{0:T(1024)S(1)} %pad_clamp_fusion), kind=kCustom, calls=%fused_computation.1 | custom fusion | bytes 8389120 | tf_op jit(solution)/shard_map/gather | solution.py:19
  276.2 71.0 %reduce-scatter.8.cloned.1.call-done = f32[512,128]{1,0:T(8,128)} async-done(((f32[8192,128]{1,0:T(8,128)}), f32[512,128]{1,0:T(8,128)}) %reduce-scatter.8.cloned.1.call-update) | async-done | bytes 262160 | tf_op jit(solution)/shard_map/reduce_scatter | solution.py:38
  347.3 1.8 fusion.9
  349.1 5.5 %fusion = f32[4,128,128,1]{2,1,3,0:T(8,128)} fusion(bf16[4,32,128,128]{3,2,1,0:T(8,128)(2,1)} %broadcast_select_fusion, bf16[4,32,128,128]{3,2,1,0:T(8,128)(2,1)} %bitcast.67, pred[4,32]{1,0:T(4,128)(4,1)S(1)} %compare_and_fusion), kind=kOutput, calls=%fused_computation.2 | convolution fusion | flops 538968064 | bytes 8650880 | tf_op jit(solution)/shard_map/rkij,rkjf->rif/dot_general | solution.py:21
  354.6 87.5 %all-reduce.3.cloned.1.call-done = (bf16[256,128]{0,1:T(8,128)(2,1)}, bf16[256,128]{1,0:T(8,128)(2,1)}) async-done(((bf16[256,128]{0,1:T(8,128)(2,1)}, bf16[256,128]{1,0:T(8,128)(2,1)}), (bf16[256,128]{0,1:T(8,128)(2,1)}, bf16[256,128]{1,0:T(8,128)(2,1)})) %all-reduce.3.cloned.1.call-update) | async-done | bytes 131088 | tf_op jit(solution)/shard_map/psum | solution.py:49
  (37 shorter events, 10.6 us)
Async XLA Ops:
  7.2 72.7 %copy-start = (bf16[512,128]{1,0:T(8,128)(2,1)S(1)}, bf16[512,128]{1,0:T(8,128)(2,1)}, u32[]{:S(2)}) copy-start(bf16[512,128]{1,0:T(8,128)(2,1)} %param.13) | copy-start | bytes 393220
  7.2 60.3 %all-gather.4.cloned.1.call-start = ((), (), s32[]{:S(2)}) async-start(), calls=%async_computation.3 | async-start | bytes 6291456 | tf_op jit(solution)/shard_map/all_gather | solution.py:53
  7.9 156.0 %reduce-scatter.4.cloned.1.call-start = ((), (), s32[]{:S(2)}) async-start(), calls=%async_computation.6 | async-start | bytes 4456448 | tf_op jit(solution)/shard_map/reduce_scatter | solution.py:38
  79.9 3.4 copy-start.5
  91.7 0.9 copy-start.2
  91.7 6.7 %copy-start.4 = (bf16[256,256]{1,0:T(8,128)(2,1)S(1)}, bf16[256,256]{1,0:T(8,128)(2,1)}, u32[]{:S(2)}) copy-start(bf16[256,256]{1,0:T(8,128)(2,1)} %param.8) | copy-start | bytes 393220
  91.7 72.2 %copy-start.3 = (bf16[256,256]{1,0:T(8,128)(2,1)S(1)}, bf16[256,256]{1,0:T(8,128)(2,1)}, u32[]{:S(2)}) copy-start(bf16[256,256]{1,0:T(8,128)(2,1)} %param.9) | copy-start | bytes 393220
  91.7 115.1 %all-gather.6.cloned.1.call-start = ((), (), s32[]{:S(2)}) async-start(), calls=%async_computation.4 | async-start | bytes 2228224 | tf_op jit(solution)/shard_map/all_gather | solution.py:16
  99.3 124.0 %reduce-scatter.6.cloned.1.call-start = ((), (), s32[]{:S(2)}) async-start(), calls=%async_computation.7 | async-start | bytes 786432 | tf_op jit(solution)/shard_map/reduce_scatter | solution.py:77
  165.9 105.6 %all-gather.8.cloned.1.call-start = ((), (), s32[]{:S(2)}) async-start(), calls=%async_computation.5 | async-start | bytes 2228224 | tf_op jit(solution)/shard_map/all_gather | solution.py:16
  231.1 116.2 %reduce-scatter.8.cloned.1.call-start = ((), (), s32[]{:S(2)}) async-start(), calls=%async_computation.8 | async-start | bytes 4456448 | tf_op jit(solution)/shard_map/reduce_scatter | solution.py:38
  243.1 0.9 copy-start.1
  243.1 199.0 %all-reduce.3.cloned.1.call-start = ((), (), s32[]{:S(2)}) async-start(), calls=%async_computation.9 | async-start | bytes 262144 | tf_op jit(solution)/shard_map/psum | solution.py:49
Sparse Core Ops, SparseCore 0:
  9.5 57.8 all-gather.3
  91.8 72.0 reduce-scatter.3
  166.7 40.0 all-gather.5
  208.8 14.4 reduce-scatter.5
  231.2 40.2 all-gather.7
  275.3 71.9 reduce-scatter.7
  351.4 90.6 all-reduce.2
where the time goes:
time: 453 us; the launch traced here: 452 us
  waiting for transfers between devices  355 us (78%)
  matrix products  31.6 us (7%)
  local copies, waits for them, and re-layouts  31 us (7%)
  between operations  14.2 us (3%)
  blocking collectives  11.6 us (3%)
  other arithmetic  7.83 us (2%)
    reduce_scatter x2, waiting for transfers between devices, backward_scatter(): lax.psum_scatter(summed.reshape(count, width), 'dom', scatter_dimension=0...  136 us
    psum x1, waiting for transfers between devices, weight_grad(): lax.psum(jnp.dot(full.T, back, preferred_element_type=jnp.float32).astype...  87.5 us
    all_gather x2, waiting for transfers between devices, forward_fold(): piece = lax.all_gather(prod, 'dom', axis=0, tiled=True)  67.3 us
    all_gather x1, waiting for transfers between devices, body(): all_vals = lax.all_gather(block_vals, 'col', axis=1, tiled=True)  58.8 us
    all_gather x2, blocking collectives, widen(): return lax.all_gather(value, 'col', axis=1, tiled=True)  11.6 us
    dot_general x2, matrix products, forward_fold(): jnp.einsum('rkij,rkjf->rif', vals, picked, preferred_element_type=jnp.flo...  10.4 us
  transfers between devices with their start and end apart: 7, of which 7 were waited for; matrix products, arithmetic and copies ran while one was open for 8% of the time, Pallas kernels for 0%

commit v1 on v0

--- a/solution.py
+++ b/solution.py
@@ -46,8 +46,12 @@
         return lax.all_gather(value, "col", axis=1, tiled=True)
 
     def weight_grad(full, back):
-        return lax.psum(
-            jnp.dot(full.T, back, preferred_element_type=jnp.float32).astype(jnp.bfloat16), "dom"
+        return jnp.sum(
+            lax.all_gather(
+                jnp.dot(full.T, back, preferred_element_type=jnp.float32).astype(jnp.bfloat16),
+                "dom",
+            ),
+            axis=0,
         ).astype(jnp.float32)
 
     all_vals = lax.all_gather(block_vals, "col", axis=1, tiled=True)

time: 453 us -> 441 us (0.974)
  waiting for transfers between devices: 355 us -> 341 us
    psum x1 -> x0, waiting for transfers between devices: 87.5 us -> none  [weight_grad(): lax.psum(jnp.dot(full.T, back, preferred_element_type=jnp.float32).astype...]
    all_gather x0 -> x2, waiting for transfers between devices: none -> 65.8 us  [weight_grad(): lax.all_gather(jnp.dot(full.T, back, preferred_element_type=jnp.float32)....]
    all_gather x2, waiting for transfers between devices: 67.3 us -> 81.4 us  [forward_fold(): piece = lax.all_gather(prod, 'dom', axis=0, tiled=True)]
    reduce_scatter x2, waiting for transfers between devices: 136 us -> 129 us  [backward_scatter(): lax.psum_scatter(summed.reshape(count, width), 'dom', scatter_dimension=0...]
  transfers between devices with their start and end apart: 7 -> 8, of which waited for: 7 -> 8; matrix products, arithmetic and copies ran while one was open for 8% -> 7% of each run, Pallas kernels for 0% -> 0%
where the time goes in v1:
time: 441 us; the launch traced here: 439 us
  waiting for transfers between devices  341 us (77%)
  matrix products  31.7 us (7%)
  local copies, waits for them, and re-layouts  30.8 us (7%)
  between operations  14.2 us (3%)
  blocking collectives  11.6 us (3%)
  other arithmetic  8.89 us (2%)
    reduce_scatter x2, waiting for transfers between devices, backward_scatter(): lax.psum_scatter(summed.reshape(count, width), 'dom', scatter_dimension=0...  129 us
    all_gather x2, waiting for transfers between devices, forward_fold(): piece = lax.all_gather(prod, 'dom', axis=0, tiled=True)  81.4 us
    all_gather x2, waiting for transfers between devices, weight_grad(): lax.all_gather(jnp.dot(full.T, back, preferred_element_type=jnp.float32)....  65.8 us
    all_gather x1, waiting for transfers between devices, body(): all_vals = lax.all_gather(block_vals, 'col', axis=1, tiled=True)  58.8 us
    all_gather x2, blocking collectives, widen(): return lax.all_gather(value, 'col', axis=1, tiled=True)  11.6 us
    dot_general x2, matrix products, forward_fold(): jnp.einsum('rkij,rkjf->rif', vals, picked, preferred_element_type=jnp.flo...  10.5 us
  transfers between devices with their start and end apart: 8, of which 8 were waited for; matrix products, arithmetic and copies ran while one was open for 7% of the time, Pallas kernels for 0%

profile of v1, /device:TPU:8, one launch (start us, length us, event | category | flops | bytes accessed | tf_op | source)
XLA Modules:
  0.0 439.0 jit_solution(6425169477652479655)
XLA Ops:
  8.7 58.8 %all-gather.8.cloned.1.call-done = bf16[4,32,128,128]{3,2,1,0:T(8,128)(2,1)} async-done(((bf16[4,16,128,128]{3,2,1,0:T(8,128)(2,1)}), bf16[4,32,128,128]{3,2,1,0:T(8,128)(2,1)}) %all-gather.8.cloned.1.call-update) | async-done | bytes 4194320 | tf_op jit(solution)/shard_map/all_gather | solution.py:57
  67.4 4.5 %broadcast_select_fusion = bf16[4,32,128,128]{3,2,1,0:T(8,128)(2,1)} fusion(bf16[4,32,128,128]{3,2,1,0:T(8,128)(2,1)} %all-gather.8.cloned.1.call-done, pred[4,32]{1,0:T(4,128)(4,1)S(1)} %iota_compare_fusion.1), kind=kLoop, calls=%fused_computation.8 | loop fusion | flops 2097152 | bytes 8388736 | tf_op jit(solution)/shard_map/jit(_where)/select_n | solution.py:60
  72.0 7.9 %copy.17 = bf16[4,32,128,128]{2,1,0,3:T(8,128)(2,1)} copy(bf16[4,32,128,128]{3,2,1,0:T(8,128)(2,1)} %broadcast_select_fusion) | data formatting | bytes 8388608 | tf_op jit(solution)/shard_map/jit(_where)/select_n | solution.py:60
  79.9 3.4 fusion.31
  83.4 3.9 convolution_bitcast_fusion.1
  87.3 4.4 %copy.16 = f32[64,128,128]{2,1,0:T(8,128)} copy(f32[64,128,128]{2,0,1:T(8,128)S(1)} %convolution_bitcast_fusion.1) | data formatting | bytes 8388608 | tf_op jit(solution)/shard_map/rkp,rkjf->pjf/dot_general | solution.py:37
  92.6 5.8 %all_gather.28 = bf16[512,256]{1,0:T(8,128)(2,1)S(1)} all-gather(bf16[512,128]{1,0:T(8,128)(2,1)S(1)} %copy-done.3), channel_id=1, replica_groups=mesh['dom'=16,'col'=2] {'col'}, dimensions={1}, use_global_device_ids=true | all-gather | bytes 393216 | tf_op jit(solution)/shard_map/all_gather | solution.py:46
  99.3 64.7 %reduce-scatter.4.cloned.1.call-done = f32[512,128]{1,0:T(8,128)} async-done(((f32[8192,128]{1,0:T(8,128)}), f32[512,128]{1,0:T(8,128)}) %reduce-scatter.4.cloned.1.call-update) | async-done | bytes 262160 | tf_op jit(solution)/shard_map/reduce_scatter | solution.py:38
  164.1 2.0 fusion.16
  166.4 40.4 %all-gather.10.cloned.1.call-done = bf16[8192,128]{0,1:T(8,128)(2,1)} async-done(((bf16[512,128]{0,1:T(8,128)(2,1)}), bf16[8192,128]{0,1:T(8,128)(2,1)}) %all-gather.10.cloned.1.call-update) | async-done | bytes 2097168 | tf_op jit(solution)/shard_map/all_gather | solution.py:16
  206.8 3.2 copy.24
  210.0 3.1 gather_fusion
  213.1 5.0 %fusion.2 = f32[4,128,128,1]{2,1,3,0:T(8,128)S(1)} fusion(bf16[4,32,128,128]{3,2,1,0:T(8,128)(2,1)} %broadcast_select_fusion, bf16[4,32,128,128]{3,2,1,0:T(8,128)(2,1)} %bitcast.74, pred[4,32]{1,0:T(4,128)(4,1)S(1)} %compare_and_fusion), kind=kOutput, calls=%fused_computation.4 | convolution fusion | flops 538968064 | bytes 8650880 | tf_op jit(solution)/shard_map/rkij,rkjf->rif/dot_general | solution.py:21
  218.1 5.3 %reduce-scatter.6.cloned.1.call-done = f32[512,128]{1,0:T(8,128)} async-done(((f32[512,256]{1,0:T(8,128)}), f32[512,128]{1,0:T(8,128)}) %reduce-scatter.6.cloned.1.call-update) | async-done | bytes 262160 | tf_op jit(solution)/shard_map/reduce_scatter | solution.py:81
  224.4 3.4 fusion.32
  227.9 3.9 convolution_bitcast_fusion
  231.8 4.4 %copy.18 = f32[64,128,128]{2,1,0:T(8,128)} copy(f32[64,128,128]{2,0,1:T(8,128)S(1)} %convolution_bitcast_fusion) | data formatting | bytes 8388608 | tf_op jit(solution)/shard_map/rkp,rkjf->pjf/dot_general | solution.py:37
  236.3 5.8 %all_gather.30 = bf16[512,256]{1,0:T(8,128)(2,1)S(1)} all-gather(bf16[512,128]{1,0:T(8,128)(2,1)S(1)} %get-tuple-element.7), channel_id=1, replica_groups=mesh['dom'=16,'col'=2] {'col'}, dimensions={1}, use_global_device_ids=true | all-gather | bytes 393216 | tf_op jit(solution)/shard_map/all_gather | solution.py:46
  244.3 64.3 %reduce-scatter.8.cloned.1.call-done = f32[512,128]{1,0:T(8,128)} async-done(((f32[8192,128]{1,0:T(8,128)}), f32[512,128]{1,0:T(8,128)}) %reduce-scatter.8.cloned.1.call-update) | async-done | bytes 262160 | tf_op jit(solution)/shard_map/reduce_scatter | solution.py:38
  310.4 37.3 %all-gather.16.cloned.1.call-done = bf16[4096,128]{1,0:T(8,128)(2,1)} async-done(((bf16[256,128]{1,0:T(8,128)(2,1)}), bf16[4096,128]{1,0:T(8,128)(2,1)}) %all-gather.16.cloned.1.call-update) | async-done | bytes 1048592 | tf_op jit(solution)/shard_map/all_gather | solution.py:50
  349.7 41.0 %all-gather.12.cloned.1.call-done = bf16[8192,128]{1,0:T(8,128)(2,1)} async-done(((bf16[512,128]{1,0:T(8,128)(2,1)}), bf16[8192,128]{1,0:T(8,128)(2,1)}) %all-gather.12.cloned.1.call-update) | async-done | bytes 2097168 | tf_op jit(solution)/shard_map/all_gather | solution.py:16
  390.8 4.6 %gather_fusion.1 = bf16[128,128,128]{2,1,0:T(8,128)(2,1)} fusion(bf16[64,128,128]{2,1,0:T(8,128)(2,1)} %bitcast.72, s32[1024]{0:T(1024)S(1)} %pad_clamp_fusion), kind=kCustom, calls=%fused_computation.1 | custom fusion | bytes 8389120 | tf_op jit(solution)/shard_map/gather | solution.py:19
  395.4 5.5 %fusion = f32[4,128,128,1]{2,1,3,0:T(8,128)} fusion(bf16[4,32,128,128]{3,2,1,0:T(8,128)(2,1)} %broadcast_select_fusion, bf16[4,32,128,128]{3,2,1,0:T(8,128)(2,1)} %bitcast.73, pred[4,32]{1,0:T(4,128)(4,1)S(1)} %compare_and_fusion), kind=kOutput, calls=%fused_computation.2 | convolution fusion | flops 538968064 | bytes 8650880 | tf_op jit(solution)/shard_map/rkij,rkjf->rif/dot_general | solution.py:21
  400.9 28.5 %all-gather.14.cloned.1.call-done = bf16[4096,128]{0,1:T(8,128)(2,1)} async-done(((bf16[256,128]{0,1:T(8,128)(2,1)}), bf16[4096,128]{0,1:T(8,128)(2,1)}) %all-gather.14.cloned.1.call-update) | async-done | bytes 1048592 | tf_op jit(solution)/shard_map/all_gather | solution.py:50
  (45 shorter events, 13.6 us)
Async XLA Ops:
  7.2 72.7 %copy-start = (bf16[512,128]{1,0:T(8,128)(2,1)S(1)}, bf16[512,128]{1,0:T(8,128)(2,1)}, u32[]{:S(2)}) copy-start(bf16[512,128]{1,0:T(8,128)(2,1)} %param.13) | copy-start | bytes 393220
  7.2 60.3 %all-gather.8.cloned.1.call-start = ((), (), s32[]{:S(2)}) async-start(), calls=%async_computation.3 | async-start | bytes 6291456 | tf_op jit(solution)/shard_map/all_gather | solution.py:57
  7.9 156.2 %reduce-scatter.4.cloned.1.call-start = ((), (), s32[]{:S(2)}) async-start(), calls=%async_computation.6 | async-start | bytes 4456448 | tf_op jit(solution)/shard_map/reduce_scatter | solution.py:38
  79.9 3.4 copy-start.6
  91.7 0.9 copy-start.3
  91.7 6.7 %copy-start.5 = (bf16[256,256]{1,0:T(8,128)(2,1)S(1)}, bf16[256,256]{1,0:T(8,128)(2,1)}, u32[]{:S(2)}) copy-start(bf16[256,256]{1,0:T(8,128)(2,1)} %param.8) | copy-start | bytes 393220
  91.7 72.4 %copy-start.4 = (bf16[256,256]{1,0:T(8,128)(2,1)S(1)}, bf16[256,256]{1,0:T(8,128)(2,1)}, u32[]{:S(2)}) copy-start(bf16[256,256]{1,0:T(8,128)(2,1)} %param.9) | copy-start | bytes 393220
  91.7 115.1 %all-gather.10.cloned.1.call-start = ((), (), s32[]{:S(2)}) async-start(), calls=%async_computation.4 | async-start | bytes 2228224 | tf_op jit(solution)/shard_map/all_gather | solution.py:16
  99.3 124.1 %reduce-scatter.6.cloned.1.call-start = ((), (), s32[]{:S(2)}) async-start(), calls=%async_computation.7 | async-start | bytes 786432 | tf_op jit(solution)/shard_map/reduce_scatter | solution.py:81
  166.1 142.5 %reduce-scatter.8.cloned.1.call-start = ((), (), s32[]{:S(2)}) async-start(), calls=%async_computation.8 | async-start | bytes 4456448 | tf_op jit(solution)/shard_map/reduce_scatter | solution.py:38
  236.2 5.9 %copy-start.2 = (f32[512,128]{1,0:T(8,128)S(1)}, f32[512,128]{1,0:T(8,128)}, u32[]{:S(2)}) copy-start(f32[512,128]{1,0:T(8,128)} %reduce-scatter.4.cloned.1.call-done) | copy-start | bytes 786436
  236.2 111.5 %all-gather.16.cloned.1.call-start = ((), (), s32[]{:S(2)}) async-start(), calls=%async_computation.10 | async-start | bytes 1114112 | tf_op jit(solution)/shard_map/all_gather | solution.py:50
  243.0 147.7 %all-gather.12.cloned.1.call-start = ((), (), s32[]{:S(2)}) async-start(), calls=%async_computation.5 | async-start | bytes 2228224 | tf_op jit(solution)/shard_map/all_gather | solution.py:16
  244.0 185.4 %all-gather.14.cloned.1.call-start = ((), (), s32[]{:S(2)}) async-start(), calls=%async_computation.9 | async-start | bytes 1114112 | tf_op jit(solution)/shard_map/all_gather | solution.py:50
  395.4 36.8 %copy-start.1 = (bf16[512,128]{1,0:T(8,128)(2,1)S(1)}, bf16[512,128]{1,0:T(8,128)(2,1)}, u32[]{:S(2)}) copy-start(bf16[512,128]{1,0:T(8,128)(2,1)} %param.13) | copy-start | bytes 393220
Sparse Core Ops, SparseCore 0:
  9.5 57.8 all-gather.7
  91.9 72.1 reduce-scatter.3
  166.8 39.9 all-gather.9
  208.9 14.4 reduce-scatter.5
  236.4 72.1 reduce-scatter.7
  311.2 36.4 all-gather.15
  350.4 40.2 all-gather.11
  392.9 36.4 all-gather.13
